TPU v7x, 128 devices: a whole 4x4x4 slice. The times are simulated.
128 devices in a mesh: lon: 32 (over y, z, x_lo), ch: 4 (over x_hi, core).
Axes of the slice: x: 4 (x_hi: 2, x_lo: 2; x = x_hi * 2 + x_lo), y: 4, z: 4, core: 2. Of those that a mesh axis runs over, the one named last changes fastest.
Arguments:
- features: bfloat16 [1024, 1, 576, 128], P('ch', None, 'lon'), may hold values from -6 to 6
- cotangent: bfloat16 [3, 256, 1, 576, 128], P(None, 'ch', None, 'lon'), may hold values from -6 to 6
- weights: bfloat16 [3, 3, 3, 256, 1024], P(None, None, None, 'ch'), may hold values from -0.0625 to 0.0625
Outputs:
- input_grad: bfloat16 [1024, 1, 576, 128], P('ch', None, 'lon')
- kernel_grad: float32 [3, 3, 3, 256, 1024], P(None, None, None, 'ch')
All inputs are finite; a program needn't handle non-finite values.
Results may differ from a plain program's by a relative error of at most 0.001.
Values may be sent and summed in bfloat16 or wider, within the bound.
A program may use at most 256 MiB of HBM per device.

v0:
```python
import jax
import jax.numpy as jnp
from jax import lax
from jax.sharding import PartitionSpec as P

DILATIONS = (6, 12, 18)
RIM = 18


def with_halo(cells, sides, width):
    for axis, dim in sides:
        count = lax.axis_size(axis)
        head = lax.slice_in_dim(cells, 0, width, axis=dim)
        tail = lax.slice_in_dim(cells, cells.shape[dim] - width, cells.shape[dim], axis=dim)
        cells = jnp.concatenate(
            [
                lax.ppermute(tail, axis, [(i, (i + 1) % count) for i in range(count)]),
                cells,
                lax.ppermute(head, axis, [((i + 1) % count, i) for i in range(count)]),
            ],
            axis=dim,
        )
    return cells


def filter_terms(cotangent, widened):
    lon_cols = cotangent.shape[3]
    lat_rows = cotangent.shape[4]
    padded = jnp.pad(widened, ((0, 0), (0, 0), (0, 0), (RIM, RIM)))
    results = []
    for branch in range(3):
        dilation = DILATIONS[branch]
        for lat_tap in range(3):
            for lon_tap in range(3):
                lon_start = RIM + dilation * (lon_tap - 1)
                lat_start = RIM + dilation * (lat_tap - 1)
                window = padded[
                    :, :, lon_start : lon_start + lon_cols, lat_start : lat_start + lat_rows
                ]
                results.append(
                    lax.dot_general(
                        cotangent[branch],
                        window,
                        (((1, 2, 3), (1, 2, 3)), ((), ())),
                        preferred_element_type=jnp.float32,
                    )
                )
    stacked = jnp.stack(results)
    return stacked.reshape(3, 3, 3, stacked.shape[1], stacked.shape[2])


def branch_taps(grad_ext, offset, dilation, lon_cols, lat_rows):
    grad_pad = jnp.pad(grad_ext, ((0, 0), (0, 0), (0, 0), (dilation, dilation)))
    slices = []
    for lat_tap in range(3):
        for lon_tap in range(3):
            lon_start = offset - dilation * (lon_tap - 1)
            lat_start = dilation - dilation * (lat_tap - 1)
            slices.append(
                grad_pad[:, :, lon_start : lon_start + lon_cols, lat_start : lat_start + lat_rows]
            )
    return jnp.concatenate(slices, axis=0)


def local(features, cotangent, weights):
    in_rows = features.shape[0]
    in_total = weights.shape[4]
    samples = features.shape[1]
    lon_cols = features.shape[2]
    lat_rows = features.shape[3]
    cells_here = samples * lon_cols * lat_rows
    whole = lax.all_gather(features, "ch", axis=0, tiled=True)
    widened = with_halo(whole, (("lon", 2),), RIM)
    partial_kernel = filter_terms(cotangent, widened)
    cells_all = cells_here * lax.axis_size("lon")
    kernel_grad = lax.psum(partial_kernel, "lon") / jnp.sqrt(jnp.float32(cells_all))
    grad_wide = with_halo(cotangent, (("lon", 3),), RIM)
    extended = [grad_wide[0], grad_wide[1], grad_wide[2]]
    offsets = [RIM, RIM, RIM]
    grad_stack = jnp.concatenate(
        [branch_taps(extended[k], offsets[k], DILATIONS[k], lon_cols, lat_rows) for k in range(3)],
        axis=0,
    ).reshape(-1, cells_here)
    kernel_matrix = weights.reshape(-1, in_total)
    product = lax.dot_general(
        kernel_matrix, grad_stack, (((0,), (0,)), ((), ())), preferred_element_type=jnp.float32
    )
    input_grad = lax.psum_scatter(
        product.reshape(lax.axis_size("ch") * in_rows, samples, lon_cols, lat_rows),
        "ch",
        scatter_dimension=0,
        tiled=True,
    ).astype(jnp.bfloat16)
    return (input_grad, kernel_grad)


def solution(mesh):
    return jax.shard_map(
        local,
        mesh=mesh,
        in_specs=(
            P("ch", None, "lon", None),
            P(None, "ch", None, "lon", None),
            P(None, None, None, "ch", None),
        ),
        out_specs=(P("ch", None, "lon", None), P(None, None, None, "ch", None)),
        check_vma=False,
    )
```

profile of v0, /device:TPU:1, one launch (start us, length us, event | category | flops | bytes accessed | tf_op | source)
XLA Modules:
  0.0 891.6 jit_solution(3159787470432086120)
XLA Ops:
  8.0 46.9 %all-gather.2.cloned.1.call-done = bf16[1024,1,18,128]{3,0,2,1:T(8,128)(2,1)} async-done(((bf16[256,1,18,128]{3,0,2,1:T(8,128)(2,1)}), bf16[1024,1,18,128]{3,0,2,1:T(8,128)(2,1)}) %all-gather.2.cloned.1.call-update) | async-done | bytes 4718608 | tf_op jit(solution)/shard_map/all_gather | solution.py:72
  54.8 4.9 collective-permute-start.3
  59.7 5.7 collective-permute-start.1
  65.4 217.4 %collective-permute-done = bf16[3,64,1,18,128]{4,1,3,2,0:T(8,128)(2,1)S(1)} collective-permute-done((bf16[3,64,1,18,128]{4,1,3,2,0:T(8,128)(2,1)}, bf16[3,64,1,18,128]{4,1,3,2,0:T(8,128)(2,1)S(1)}, u32[]{:S(2)}, u32[]{:S(2)}) %collective-permute-start) | collective-permute-done | bytes 884768 | tf_op jit(solution)/shard_map/ppermute | solution.py:17
  283.9 21.6 %fusion.5 = bf16[1024,1,54,164]{3,0,2,1:T(8,128)(2,1)} fusion(bf16[1024,1,18,128]{3,0,2,1:T(8,128)(2,1)} %collective-permute-done.3, bf16[1024,1,18,128]{3,0,2,1:T(8,128)(2,1)} %all-gather.2.cloned.1.call-done, bf16[1024,1,18,128]{3,0,2,1:T(8,128)(2,1)} %collective-permute-done.2), kind=kLoop, calls=%fused_computation.7 | loop fusion | flops 108822528 | bytes 32292864 | tf_op jit(solution)/shard_map/concatenate | solution.py:15
  305.6 5.9 fusion.69
  311.5 6.0 fusion.71
  317.4 5.9 fusion.73
  323.3 4.8 constant_dynamic-update-slice_fusion.4
  328.2 5.8 constant_dynamic-update-slice_fusion.6
  333.9 4.0 fusion.75
  345.1 5.8 fusion.79
  350.9 6.0 fusion.81
  357.0 5.8 fusion.83
  362.8 5.8 fusion.85
  368.6 6.0 fusion.87
  374.6 5.9 fusion.89
  385.1 6.2 fusion.95
  391.3 5.8 fusion.97
  397.2 5.8 fusion.99
  403.0 4.0 fusion.101
  407.0 4.0 fusion.103
  411.1 4.0 fusion.105
  415.1 4.0 fusion.59
  420.6 4.0 fusion.65
  424.7 6.0 fusion.107
  468.2 11.9 %copy.6 = bf16[1728,1,18,128]{0,3,2,1:T(8,128)(2,1)} copy(bf16[1728,1,18,128]{3,0,2,1:T(8,128)(2,1)} %fusion.129) | data formatting | bytes 15925248 | tf_op jit(solution)/shard_map/concatenate | solution.py:80
  480.1 13.2 %fusion.184 = f32[2304,1024]{1,0:T(8,128)} fusion(bf16[1728,2304]{0,1:T(8,128)(2,1)} %bitcast.465, bf16[1728,1024]{1,0:T(8,128)(2,1)S(1)} %bitcast.459), kind=kOutput, calls=%fused_computation.226 | convolution fusion | flops 8153726976 | bytes 20938752 | tf_op jit(solution)/shard_map/dot_general | solution.py:85
  493.3 9.7 %copy.7 = f32[1024,1,18,128]{3,0,2,1:T(8,128)} copy(f32[1024,1,18,128]{0,3,2,1:T(8,128)} %bitcast.464) | data formatting | bytes 18874368 | tf_op jit(solution)/shard_map/reshape | solution.py:89
  503.0 276.2 %all-reduce.6.cloned.1.call-done = f32[3,3,3,64,1024]{4,3,2,1,0:T(8,128)} async-done(((f32[3,3,3,64,1024]{4,3,2,1,0:T(8,128)}), f32[3,3,3,64,1024]{4,3,2,1,0:T(8,128)}) %all-reduce.6.cloned.1.call-update) | async-done | bytes 7077904 | tf_op jit(solution)/shard_map/psum | solution.py:76
  779.2 7.6 broadcast_multiply_fusion
  786.8 95.1 %reduce-scatter.2.cloned.1.call-done = f32[256,1,18,128]{3,0,2,1:T(8,128)} async-done(((f32[1024,1,18,128]{3,0,2,1:T(8,128)}), f32[256,1,18,128]{3,0,2,1:T(8,128)}) %reduce-scatter.2.cloned.1.call-update) | async-done | bytes 2359312 | tf_op jit(solution)/shard_map/reduce_scatter | solution.py:88
  (87 shorter events, 55.6 us)
Async XLA Ops:
  7.2 472.9 %copy-start = (bf16[3,3,3,64,1024]{4,3,2,1,0:T(8,128)(2,1)S(1)}, bf16[3,3,3,64,1024]{4,3,2,1,0:T(8,128)(2,1)}, u32[]{:S(2)}) copy-start(bf16[3,3,3,64,1024]{4,3,2,1,0:T(8,128)(2,1)} %param.5) | copy-start | bytes 10616836
  7.2 47.6 %all-gather.2.cloned.1.call-start = ((), (), s32[]{:S(2)}) async-start(), calls=%async_computation.2 | async-start | bytes 5898240 | tf_op jit(solution)/shard_map/all_gather | solution.py:72
  7.9 771.2 %all-reduce.6.cloned.1.call-start = ((), (), s32[]{:S(2)}) async-start(), calls=%async_computation.3 | async-start | bytes 14155776 | tf_op jit(solution)/shard_map/psum | solution.py:76
  54.8 229.1 %collective-permute-start.3 = (bf16[1024,1,18,128]{3,0,2,1:T(8,128)(2,1)}, bf16[1024,1,18,128]{3,0,2,1:T(8,128)(2,1)}, u32[]{:S(2)}, u32[]{:S(2)}) collective-permute-start(bf16[1024,1,18,128]{3,0,2,1:T(8,128)(2,1)} %all-gather.2.cloned.1.call-done), channel_id=1, source_target_pairs={{4,0},{8,4},{12,8},{16,12},{20,16},{24,20},{28,24},{32,28},{36,32}... | collective-permute-start | bytes 14155784 | tf_op jit(solution)/shard_map/ppermute | solution.py:19
  59.7 224.2 %collective-permute-start.2 = (bf16[1024,1,18,128]{3,0,2,1:T(8,128)(2,1)}, bf16[1024,1,18,128]{3,0,2,1:T(8,128)(2,1)}, u32[]{:S(2)}, u32[]{:S(2)}) collective-permute-start(bf16[1024,1,18,128]{3,0,2,1:T(8,128)(2,1)} %all-gather.2.cloned.1.call-done), channel_id=1, source_target_pairs={{0,4},{4,8},{8,12},{12,16},{16,20},{20,24},{24,28},{28,32},{32,36}... | collective-permute-start | bytes 14155784 | tf_op jit(solution)/shard_map/ppermute | solution.py:17
  59.7 223.1 %collective-permute-start = (bf16[3,64,1,18,128]{4,1,3,2,0:T(8,128)(2,1)}, bf16[3,64,1,18,128]{4,1,3,2,0:T(8,128)(2,1)S(1)}, u32[]{:S(2)}, u32[]{:S(2)}) collective-permute-start(bf16[3,64,1,18,128]{4,1,3,2,0:T(8,128)(2,1)} %param.4), channel_id=1, source_target_pairs={{0,4},{4,8},{8,12},{12,16},{16,20},{20,24},{24,28},{28,32},{32,36}... | collective-permute-start | bytes 2654216 | tf_op jit(solution)/shard_map/ppermute | solution.py:17
  59.7 380.8 %collective-permute-start.1 = (bf16[3,64,1,18,128]{4,1,3,2,0:T(8,128)(2,1)}, bf16[3,64,1,18,128]{4,1,3,2,0:T(8,128)(2,1)}, u32[]{:S(2)}, u32[]{:S(2)}) collective-permute-start(bf16[3,64,1,18,128]{4,1,3,2,0:T(8,128)(2,1)} %param.4), channel_id=1, source_target_pairs={{4,0},{8,4},{12,8},{16,12},{20,16},{24,20},{28,24},{32,28},{36,32}... | collective-permute-start | bytes 2654216 | tf_op jit(solution)/shard_map/ppermute | solution.py:19
  305.5 5.9 copy-start.2
  311.4 16.7 %slice-start = ((s8[4718592]{0:T(1024)(128)(4,1)}), s8[4194304]{0:T(1024)(128)(4,1)S(1)}, s32[]{:S(2)}) async-start(s8[4718592]{0:T(1024)(128)(4,1)} %bitcast.460), calls=%async_computation.4 | async-start | bytes 8388608
  317.4 10.7 %slice-start.1 = ((s8[4718592]{0:T(1024)(128)(4,1)}), s8[524288]{0:T(1024)(128)(4,1)S(1)}, s32[]{:S(2)}) async-start(s8[4718592]{0:T(1024)(128)(4,1)} %bitcast.460), calls=%async_computation.5 | async-start | bytes 1048576
  333.9 5.1 copy-start.3
  368.6 11.9 %slice-start.9 = ((s8[9437184]{0:T(1024)(128)(4,1)}), s8[4194304]{0:T(1024)(128)(4,1)S(1)}, s32[]{:S(2)}) async-start(s8[9437184]{0:T(1024)(128)(4,1)} %bitcast.467), calls=%async_computation.13 | async-start | bytes 8388608
  368.6 11.9 %slice-start.10 = ((s8[9437184]{0:T(1024)(128)(4,1)}), s8[4194304]{0:T(1024)(128)(4,1)S(1)}, s32[]{:S(2)}) async-start(s8[9437184]{0:T(1024)(128)(4,1)} %bitcast.467), calls=%async_computation.14 | async-start | bytes 8388608
  374.6 5.9 slice-start.11
  403.0 27.7 %slice-start.2 = ((s8[28311552]{0:T(1024)(128)(4,1)}), s8[4194304]{0:T(1024)(128)(4,1)S(1)}, s32[]{:S(2)}) async-start(s8[28311552]{0:T(1024)(128)(4,1)} %bitcast.462), calls=%async_computation.6 | async-start | bytes 8388608
  403.0 27.7 %slice-start.3 = ((s8[28311552]{0:T(1024)(128)(4,1)}), s8[4194304]{0:T(1024)(128)(4,1)S(1)}, s32[]{:S(2)}) async-start(s8[28311552]{0:T(1024)(128)(4,1)} %bitcast.462), calls=%async_computation.7 | async-start | bytes 8388608
  407.0 23.6 %slice-start.4 = ((s8[28311552]{0:T(1024)(128)(4,1)}), s8[4194304]{0:T(1024)(128)(4,1)S(1)}, s32[]{:S(2)}) async-start(s8[28311552]{0:T(1024)(128)(4,1)} %bitcast.462), calls=%async_computation.8 | async-start | bytes 8388608
  411.0 19.6 %slice-start.5 = ((s8[28311552]{0:T(1024)(128)(4,1)}), s8[4194304]{0:T(1024)(128)(4,1)S(1)}, s32[]{:S(2)}) async-start(s8[28311552]{0:T(1024)(128)(4,1)} %bitcast.462), calls=%async_computation.9 | async-start | bytes 8388608
  415.1 15.6 %slice-start.6 = ((s8[28311552]{0:T(1024)(128)(4,1)}), s8[4194304]{0:T(1024)(128)(4,1)S(1)}, s32[]{:S(2)}) async-start(s8[28311552]{0:T(1024)(128)(4,1)} %bitcast.462), calls=%async_computation.10 | async-start | bytes 8388608
  420.6 10.1 %slice-start.7 = ((s8[28311552]{0:T(1024)(128)(4,1)}), s8[4194304]{0:T(1024)(128)(4,1)S(1)}, s32[]{:S(2)}) async-start(s8[28311552]{0:T(1024)(128)(4,1)} %bitcast.462), calls=%async_computation.11 | async-start | bytes 8388608
  424.7 6.0 slice-start.8
  435.2 3.0 copy-start.1
  438.2 443.8 %reduce-scatter.2.cloned.1.call-start = ((), (), s32[]{:S(2)}) async-start(), calls=%async_computation.1 | async-start | bytes 11796480 | tf_op jit(solution)/shard_map/reduce_scatter | solution.py:88
Sparse Core Ops, SparseCore 0:
  9.7 45.0 all-gather.1
  438.3 340.8 all-reduce.5
  781.9 100.0 reduce-scatter.1
where the time goes:
time: 896 us; the launch traced here: 892 us
  waiting for transfers between devices  636 us (71%)
  matrix products  128 us (14%)
  local copies, waits for them, and re-layouts  70.3 us (8%)
  other arithmetic  32.2 us (4%)
  between operations  14.2 us (2%)
  starting transfers between devices  10.7 us (1%)
    psum x1, waiting for transfers between devices, local(): lax.psum(partial_kernel, 'lon') / jnp.sqrt(jnp.float32(cells_all))  276 us
    ppermute x2, waiting for transfers between devices, with_halo(): lax.ppermute(tail, axis, [(i, (i + 1) % count) for i in range(count)])  217 us
    dot_general x27, matrix products, filter_terms(): lax.dot_general(cotangent[branch], window, (((1, 2, 3), (1, 2, 3)), ((),...  115 us
    reduce_scatter x1, waiting for transfers between devices, local(): lax.psum_scatter(product.reshape(lax.axis_size('ch') * in_rows, samples,...  95.1 us
    all_gather x1, waiting for transfers between devices, local(): whole = lax.all_gather(features, 'ch', axis=0, tiled=True)  46.9 us
    unnamed x62, local copies, waits for them, and re-layouts  40.3 us
    concatenate x1, other arithmetic, with_halo(): jnp.concatenate([lax.ppermute(tail, axis, [(i, (i + 1) % count) for i in...  21.6 us
  transfers between devices with their start and end apart: 7, of which 4 were waited for; matrix products, arithmetic and copies ran while one was open for 25% of the time, Pallas kernels for 0%

commit v1 on v0

--- a/solution.py
+++ b/solution.py
@@ -73,7 +73,9 @@
     widened = with_halo(whole, (("lon", 2),), RIM)
     partial_kernel = filter_terms(cotangent, widened)
     cells_all = cells_here * lax.axis_size("lon")
-    kernel_grad = lax.psum(partial_kernel, "lon") / jnp.sqrt(jnp.float32(cells_all))
+    kernel_grad = jnp.sum(lax.all_gather(partial_kernel, "lon"), axis=0) / jnp.sqrt(
+        jnp.float32(cells_all)
+    )
     grad_wide = with_halo(cotangent, (("lon", 3),), RIM)
     extended = [grad_wide[0], grad_wide[1], grad_wide[2]]
     offsets = [RIM, RIM, RIM]

time: 896 us -> 5280 us (5.89)
  waiting for transfers between devices: 636 us -> 4970 us
  other arithmetic: 32.2 us -> 103 us
    all_gather x0 -> x1, waiting for transfers between devices: none -> 4710 us  [local(): lax.all_gather(partial_kernel, 'lon')]
    psum x1 -> x0, waiting for transfers between devices: 276 us -> none  [local(): lax.psum(partial_kernel, 'lon') / jnp.sqrt(jnp.float32(cells_all))]
    ppermute x2, waiting for transfers between devices: 0.01 us -> 155 us  [with_halo(): lax.ppermute(head, axis, [((i + 1) % count, i) for i in range(count)])]
    ppermute x2, waiting for transfers between devices: 217 us -> 96 us  [with_halo(): lax.ppermute(tail, axis, [(i, (i + 1) % count) for i in range(count)])]
    reduce_scatter x1, waiting for transfers between devices: 95.1 us -> 0.02 us  [local(): lax.psum_scatter(product.reshape(lax.axis_size('ch') * in_rows, samples,...]
    reduce_sum x0 -> x1, other arithmetic: none -> 71.2 us  [local(): jnp.sum(lax.all_gather(partial_kernel, 'lon'), axis=0)]
  transfers between devices with their start and end apart: 7 -> 7, of which waited for: 4 -> 5; matrix products, arithmetic and copies ran while one was open for 25% -> 4% of each run, Pallas kernels for 0% -> 0%
where the time goes in v1:
time: 5280 us; the launch traced here: 5270 us
  waiting for transfers between devices  4970 us (94%)
  matrix products  109 us (2%)
  other arithmetic  103 us (2%)
  local copies, waits for them, and re-layouts  66.3 us (1%)
    all_gather x1, waiting for transfers between devices, local(): lax.all_gather(partial_kernel, 'lon')  4710 us
    ppermute x2, waiting for transfers between devices, with_halo(): lax.ppermute(head, axis, [((i + 1) % count, i) for i in range(count)])  155 us
  transfers between devices with their start and end apart: 7, of which 5 were waited for; matrix products, arithmetic and copies ran while one was open for 4% of the time, Pallas kernels for 0%

profile of v1, /device:TPU:1, one launch (start us, length us, event | category | flops | bytes accessed | tf_op | source)
XLA Modules:
  0.0 5273.5 jit_solution(5824418473337178762)
XLA Ops:
  10.1 6.0 collective-permute-start.1
  16.1 24.1 collective-permute-done
  41.6 31.9 collective-permute-done.1
  99.7 4.5 collective-permute-start.3
  107.9 11.6 copy.8
  119.5 13.3 fusion.184
  132.7 9.6 copy.9
  142.6 71.9 %collective-permute-done.2 = bf16[1024,1,18,128]{3,0,2,1:T(8,128)(2,1)} collective-permute-done((bf16[1024,1,18,128]{3,0,2,1:T(8,128)(2,1)}, bf16[1024,1,18,128]{3,0,2,1:T(8,128)(2,1)}, u32[]{:S(2)}, u32[]{:S(2)}) %collective-permute-start.2) | collective-permute-done | bytes 4718624 | tf_op jit(solution)/shard_map/ppermute | solution.py:17
  217.1 7.4 constant_dynamic-update-slice_fusion.6
  224.5 122.7 %collective-permute-done.3 = bf16[1024,1,18,128]{3,0,2,1:T(8,128)(2,1)} collective-permute-done((bf16[1024,1,18,128]{3,0,2,1:T(8,128)(2,1)}, bf16[1024,1,18,128]{3,0,2,1:T(8,128)(2,1)}, u32[]{:S(2)}, u32[]{:S(2)}) %collective-permute-start.3) | collective-permute-done | bytes 4718624 | tf_op jit(solution)/shard_map/ppermute | solution.py:19
  347.3 5.0 constant_dynamic-update-slice_fusion.5
  352.3 21.6 fusion.5
  373.9 6.7 fusion.69
  380.6 6.7 fusion.71
  387.2 6.7 fusion.73
  393.9 4.7 fusion.75
  400.9 4.7 fusion.77
  405.6 2.9 fusion.79
  408.5 2.9 fusion.81
  411.4 3.3 fusion.83
  414.6 2.9 fusion.85
  417.5 2.9 fusion.87
  420.4 2.9 fusion.89
  423.2 4.6 fusion.91
  430.0 4.6 fusion.93
  437.5 3.0 fusion.97
  450.1 4.6 fusion.59
  456.9 4.6 fusion.65
  470.1 2.9 convert_element_type.11
  473.0 4715.0 %all-gather.5.cloned.1.call-done = f32[32,3,3,3,64,1024]{5,4,3,2,1,0:T(8,128)} async-done(((f32[1,3,3,3,64,1024]{5,4,3,2,1,0:T(8,128)}), f32[32,3,3,3,64,1024]{5,4,3,2,1,0:T(8,128)}) %all-gather.5.cloned.1.call-update) | async-done | bytes 226492432 | tf_op jit(solution)/shard_map/all_gather | solution.py:76
  5188.0 71.2 %reduce_sum.9 = f32[3,3,3,64,1024]{4,3,2,1,0:T(8,128)} reduce(f32[32,3,3,3,64,1024]{5,4,3,2,1,0:T(8,128)} %all-gather.5.cloned.1.call-done, f32[]{:T(128)} %constant.6.clone.1), dimensions={0}, to_apply=%region_1.2 | reduce | flops 54853632 | bytes 233570304 | tf_op jit(solution)/shard_map/reduce_sum | solution.py:76
  5259.2 7.6 broadcast_multiply_fusion
  (83 shorter events, 64.7 us)
Async XLA Ops:
  7.2 112.3 %copy-start = (bf16[3,3,3,64,1024]{4,3,2,1,0:T(8,128)(2,1)S(1)}, bf16[3,3,3,64,1024]{4,3,2,1,0:T(8,128)(2,1)}, u32[]{:S(2)}) copy-start(bf16[3,3,3,64,1024]{4,3,2,1,0:T(8,128)(2,1)} %param.5) | copy-start | bytes 10616836
  7.2 85.9 %all-gather.3.cloned.1.call-start = ((), (), s32[]{:S(2)}) async-start(), calls=%async_computation.2 | async-start | bytes 5898240 | tf_op jit(solution)/shard_map/all_gather | solution.py:72
  7.9 462.2 %reduce-scatter.2.cloned.1.call-start = ((), (), s32[]{:S(2)}) async-start(), calls=%async_computation.1 | async-start | bytes 11796480 | tf_op jit(solution)/shard_map/reduce_scatter | solution.py:90
  8.0 32.3 collective-permute-start
  10.1 63.4 %collective-permute-start.1 = (bf16[3,64,1,18,128]{4,1,3,2,0:T(8,128)(2,1)}, bf16[3,64,1,18,128]{4,1,3,2,0:T(8,128)(2,1)S(1)}, u32[]{:S(2)}, u32[]{:S(2)}) collective-permute-start(bf16[3,64,1,18,128]{4,1,3,2,0:T(8,128)(2,1)} %param.4), channel_id=1, source_target_pairs={{4,0},{8,4},{12,8},{16,12},{20,16},{24,20},{28,24},{32,28},{36,32}... | collective-permute-start | bytes 2654216 | tf_op jit(solution)/shard_map/ppermute | solution.py:19
  74.2 18.1 copy-start.2
  93.1 121.3 %collective-permute-start.2 = (bf16[1024,1,18,128]{3,0,2,1:T(8,128)(2,1)}, bf16[1024,1,18,128]{3,0,2,1:T(8,128)(2,1)}, u32[]{:S(2)}, u32[]{:S(2)}) collective-permute-start(bf16[1024,1,18,128]{3,0,2,1:T(8,128)(2,1)} %all-gather.3.cloned.1.call-done), channel_id=1, source_target_pairs={{0,4},{4,8},{8,12},{12,16},{16,20},{20,24},{24,28},{28,32},{32,36}... | collective-permute-start | bytes 14155784 | tf_op jit(solution)/shard_map/ppermute | solution.py:17
  99.7 247.6 %collective-permute-start.3 = (bf16[1024,1,18,128]{3,0,2,1:T(8,128)(2,1)}, bf16[1024,1,18,128]{3,0,2,1:T(8,128)(2,1)}, u32[]{:S(2)}, u32[]{:S(2)}) collective-permute-start(bf16[1024,1,18,128]{3,0,2,1:T(8,128)(2,1)} %all-gather.3.cloned.1.call-done), channel_id=1, source_target_pairs={{4,0},{8,4},{12,8},{16,12},{20,16},{24,20},{28,24},{32,28},{36,32}... | collective-permute-start | bytes 14155784 | tf_op jit(solution)/shard_map/ppermute | solution.py:19
  142.3 5045.6 %all-gather.5.cloned.1.call-start = ((), (), s32[]{:S(2)}) async-start(), calls=%async_computation.3 | async-start | bytes 233570304 | tf_op jit(solution)/shard_map/all_gather | solution.py:76
  224.5 122.7 %copy-start.4 = (bf16[1024,1,36,128]{3,0,2,1:T(8,128)(2,1)}, bf16[1024,1,36,128]{3,0,2,1:T(8,128)(2,1)S(1)}, u32[]{:S(2)}) copy-start(bf16[1024,1,36,128]{3,0,2,1:T(8,128)(2,1)S(1)} %get-tuple-element.3) | copy-start | bytes 28311556
  352.3 21.6 copy-start.3
  373.9 31.7 slice-start.2
  373.9 31.7 slice-start.3
  380.6 25.0 slice-start.4
  387.2 18.4 slice-start.5
  387.2 18.4 slice-start.6
  393.9 4.7 slice-start
  393.9 4.7 slice-start.1
  393.9 11.7 slice-start.7
  400.9 4.8 slice-start.8
  5188.0 78.8 %copy-start.1 = (bf16[3,3,3,64,1024]{4,3,2,1,0:T(8,128)(2,1)S(1)}, bf16[3,3,3,64,1024]{4,3,2,1,0:T(8,128)(2,1)}, u32[]{:S(2)}) copy-start(bf16[3,3,3,64,1024]{4,3,2,1,0:T(8,128)(2,1)} %param.5) | copy-start | bytes 10616836
Sparse Core Ops, SparseCore 0:
  9.7 69.2 all-gather.2
  142.4 137.9 reduce-scatter.1
  470.2 4717.7 all-gather.4
